TPU v7x, 256 devices: a whole 4x4x8 slice. The times are simulated.
256 devices in a mesh: req: 16 (over z_hi, x), mp: 16 (over z_lo, y, core).
Axes of the slice: x: 4, y: 4, z: 8 (z_hi: 4, z_lo: 2; z = z_hi * 2 + z_lo), core: 2. Of those that a mesh axis runs over, the one named last changes fastest.
Arguments:
- queries: bfloat16 [2048, 4096], P('req', 'mp'), may hold values from -6 to 6
- suffix_kv: bfloat16 [2, 2048, 4096], P(None, 'req', 'mp'), may hold values from -6 to 6
- prefix_kv: bfloat16 [2, 8192, 4096], P(None, 'req', 'mp'), may hold values from -6 to 6
- resid: bfloat16 [2048, 4096], P('req', 'mp'), may hold values from -6 to 6
- ln_gain: float32 [4096], replicated, may hold values from 0.1 to 1.9
- out_weight: bfloat16 [4096, 4096], P('mp'), may hold values from -0.125 to 0.125
- up_weight: bfloat16 [4096, 8192], P(None, 'mp'), may hold values from -0.09375 to 0.09375
- down_weight: bfloat16 [8192, 4096], P('mp'), may hold values from -0.09375 to 0.09375
- lengths: int32 [16], replicated, may hold values from 1 to 128, 1024 in all
- req_group: int32 [16], replicated, may hold values from 0 to 3, as said below
- prefix_owner: int32 [16], replicated, may hold values from 0 to 15, as said below
Outputs:
- attended: bfloat16 [2048, 4096], P('req', 'mp')
- layer_out: bfloat16 [2048, 4096], P('req', 'mp')
Inputs may be any that keep to these rules, and one draw needn't show every extreme that they name: `req_group`: each of the 4 groups holds exactly 4 requests. `prefix_owner`: a permutation: every logical block is held by exactly one stored block.
All inputs are finite; a program needn't handle non-finite values.
Results may differ from a plain program's by a relative error of at most 0.029.
Values may be sent and summed in bfloat16 or wider, within the bound.
A program may use at most 128 MiB of HBM per device.

v0:
```python
import jax
import jax.numpy as jnp
from jax import lax
from jax.sharding import PartitionSpec as P

H = 32
DH = 128
KB = 512
S_MAX = 128
P_SIZE = 2048
very_negative = -1e30


def block_partial(query_rows, key_rows, value_rows, query_pos, key_pos, allowed, slopes, shared):
    if shared:
        score_form = "rqhd,khd->rqhk"
        value_form = "rqhk,khd->rqhd"
    else:
        score_form = "rqhd,rkhd->rqhk"
        value_form = "rqhk,rkhd->rqhd"
    scores = jnp.einsum(
        score_form, query_rows, key_rows, preferred_element_type=jnp.float32
    ) * float(DH) ** (-0.5)
    distance = (query_pos[:, None, None] - key_pos[None, None, :]).astype(jnp.float32)
    scores = scores - slopes[None, :, None] * distance
    masked = jnp.where(allowed, scores, very_negative)
    maxima = jnp.max(masked, axis=-1)
    weights = jnp.where(allowed, jnp.exp(masked - maxima[..., None]), 0.0)
    totals = jnp.sum(weights, axis=-1)
    rounded = weights.astype(jnp.bfloat16)
    weighted = jnp.einsum(value_form, rounded, value_rows, preferred_element_type=jnp.float32)
    return (weighted, maxima, totals)


def combine(first_part, second_part):
    peak_max = jnp.maximum(first_part[1], second_part[1])
    scale_first = jnp.exp(first_part[1] - peak_max)
    scale_second = jnp.exp(second_part[1] - peak_max)
    weighted = first_part[0] * scale_first[..., None] + second_part[0] * scale_second[..., None]
    return (weighted, peak_max, first_part[2] * scale_first + second_part[2] * scale_second)


def shards(
    queries,
    suffix_kv,
    prefix_kv,
    resid,
    ln_gain,
    out_weight,
    up_weight,
    down_weight,
    lengths,
    req_group,
    prefix_owner,
):
    row_count = queries.shape[0]
    local_req = row_count // S_MAX
    columns = queries.shape[1]
    head_count = columns // DH
    per_group = P_SIZE // KB
    first_req = lax.axis_index("req") * local_req
    col_start = lax.axis_index("mp") * columns
    my_len = lax.dynamic_slice_in_dim(lengths, first_req, local_req)
    my_group = lax.dynamic_slice_in_dim(req_group, first_req, local_req)
    head_ids = (lax.axis_index("mp") * head_count + jnp.arange(head_count)).astype(jnp.float32)
    slopes = jnp.power(2.0, -8.0 * (head_ids + 1.0) / H)
    my_query = queries.reshape(local_req, S_MAX, head_count, DH)
    suffix_local = suffix_kv.reshape(2, local_req, S_MAX, head_count, DH)
    offsets = jnp.arange(S_MAX)
    query_pos = P_SIZE + offsets
    allowed = (offsets[None, None, :] <= offsets[None, :, None]) & (
        offsets[None, None, :] < my_len[:, None, None]
    )
    own_part = block_partial(
        my_query,
        suffix_local[0],
        suffix_local[1],
        query_pos,
        query_pos,
        allowed[:, :, None, :],
        slopes,
        False,
    )
    key_offsets = jnp.arange(KB)
    shard_piece = lax.all_gather(prefix_kv, "req", axis=1, tiled=True)
    block_total = shard_piece.shape[1] // KB
    blocks_here = shard_piece.reshape(2, block_total, KB, head_count, DH)

    def fold_step(block_index, inner_state):
        logical = prefix_owner[block_index]
        same_group = my_group == logical // per_group
        base_pos = logical % per_group * KB

        def attend_block(state_in):
            fresh = block_partial(
                my_query,
                blocks_here[0, block_index],
                blocks_here[1, block_index],
                query_pos,
                base_pos + key_offsets,
                same_group[:, None, None, None],
                slopes,
                True,
            )
            return combine(state_in, fresh)

        return lax.cond(jnp.any(same_group), attend_block, lambda state_in: state_in, inner_state)

    result = lax.fori_loop(0, block_total, fold_step, own_part)
    outcome = result[0] / result[2][..., None]
    live_mask = offsets[None, :] < my_len[:, None]
    attended = (
        jnp.where(live_mask[:, :, None, None], outcome, 0.0)
        .astype(jnp.bfloat16)
        .reshape(row_count, columns)
    )
    head_term = jnp.dot(attended, out_weight, preferred_element_type=jnp.float32)
    own_columns = lax.dynamic_slice_in_dim(head_term, col_start, columns, 1) + resid.astype(
        jnp.float32
    )
    head_term = lax.dynamic_update_slice_in_dim(head_term, own_columns, col_start, 1)
    mixed_rows = lax.psum(head_term.astype(jnp.bfloat16), "mp").astype(jnp.float32)
    row_mean = jnp.mean(mixed_rows, axis=1, keepdims=True)
    centered = mixed_rows - row_mean
    variance = jnp.mean(centered * centered, axis=1, keepdims=True)
    normed = (centered * lax.rsqrt(variance + 1e-05) * ln_gain).astype(jnp.bfloat16)
    hidden = jax.nn.gelu(
        jnp.dot(normed, up_weight, preferred_element_type=jnp.float32), approximate=False
    ).astype(jnp.bfloat16)
    projected = jnp.dot(hidden, down_weight, preferred_element_type=jnp.float32)
    update = lax.psum_scatter(
        projected.astype(jnp.bfloat16), "mp", scatter_dimension=1, tiled=True
    ).astype(jnp.float32)
    mixed_own = lax.dynamic_slice_in_dim(mixed_rows, col_start, columns, 1)
    layer_out = jnp.where(live_mask.reshape(row_count)[:, None], mixed_own + update, 0.0).astype(
        jnp.bfloat16
    )
    return (attended, layer_out)


def solution(mesh):
    placed = (
        P("req", "mp"),
        P(None, "req", "mp"),
        P(None, "req", "mp"),
        P("req", "mp"),
        P(),
        P("mp", None),
        P(None, "mp"),
        P("mp", None),
        P(),
        P(),
        P(),
    )
    return jax.shard_map(
        shards,
        mesh=mesh,
        in_specs=placed,
        out_specs=(P("req", "mp"), P("req", "mp")),
        check_vma=False,
    )
```

profile of v0, /device:TPU:6, one launch (start us, length us, event | category | flops | bytes accessed | tf_op | source)
XLA Modules:
  0.0 440.7 jit_solution(7493433449119299911)
XLA Ops:
  7.2 0.7 all-gather.2.cloned.1.call-update
  8.0 1.2 dynamic_slice.35
  9.2 1.2 dynamic_slice.34
  10.4 0.9 copy.28
  11.5 0.9 fusion.121
  13.4 1.1 fusion.122
  14.9 107.0 %all-gather.2.cloned.1.call-done = bf16[2,8192,256]{2,1,0:T(8,128)(2,1)} async-done(((bf16[2,512,256]{2,1,0:T(8,128)(2,1)}), bf16[2,8192,256]{2,1,0:T(8,128)(2,1)}) %all-gather.2.cloned.1.call-update) | async-done | bytes 8388624 | tf_op jit(solution)/shard_map/all_gather | solution.py:85
  121.9 12.5 %reshape.277 = bf16[2,16,512,2,128]{4,3,2,1,0:T(2,128)(2,1)} reshape(bf16[2,8192,256]{2,1,0:T(8,128)(2,1)} %all-gather.2.cloned.1.call-done) | data formatting | bytes 16777216 | tf_op jit(solution)/shard_map/reshape | solution.py:87
  134.4 8.8 %copy.30 = bf16[2,16,512,2,128]{4,2,3,1,0:T(8,128)(2,1)} copy(bf16[2,16,512,2,128]{4,3,2,1,0:T(2,128)(2,1)} %reshape.277) | data formatting | bytes 16777216
  143.2 79.0 %while.20 = (s32[]{:T(128)}, f32[1,128,2,128]{1,3,2,0:T(8,128)S(1)}, f32[1,128,2]{1,2,0:T(2,128)S(1)}, f32[1,128,2]{1,2,0:T(2,128)S(1)}, s32[16]{0:T(128)S(1)}, ...) while((s32[]{:T(128)}, ...), condition=%wide.region_7.8_spmd.clone, body=%wide.region_2.7_spmd.clone.sunk | while | flops 68782248 | bytes 2980505 | solution.py:109
  147.0 0.6 dynamic_slice.54
  150.7 4.7 %conditional.3 = ((f32[1,128,2,128]{1,3,2,0:T(8,128)S(1)}, f32[1,128,2]{1,2,0:T(2,128)S(1)}, f32[1,128,2]{1,2,0:T(2,128)S(1)})) conditional(s32[]{:T(128)} %bitcast.111, (f32[1,128,2,128]{1,3,2,0:T(8,128)S(1)}, f32[1,128,2]{1,2,0:T(2,128)S(1)}, f32[1,128,2]{1,2,0:T(2,128)S(1)}) %tuple.96, (pred[1]{0:T(512)(128)(4,1)}, s32[]{:T(128)}, ...), branch_computations={%region_3.3_spmd, %region_4.6_spmd.clone} | conditional | flops 68782224 | bytes 2977504 | solution.py:107
  152.8 1.2 fusion.120
  154.1 1.3 fusion.10
  174.2 4.7 %conditional.3 = ((f32[1,128,2,128]{1,3,2,0:T(8,128)S(1)}, f32[1,128,2]{1,2,0:T(2,128)S(1)}, f32[1,128,2]{1,2,0:T(2,128)S(1)})) conditional(s32[]{:T(128)} %bitcast.111, (f32[1,128,2,128]{1,3,2,0:T(8,128)S(1)}, f32[1,128,2]{1,2,0:T(2,128)S(1)}, f32[1,128,2]{1,2,0:T(2,128)S(1)}) %tuple.96, (pred[1]{0:T(512)(128)(4,1)}, s32[]{:T(128)}, ...), branch_computations={%region_3.3_spmd, %region_4.6_spmd.clone} | conditional | flops 68782224 | bytes 2977504 | solution.py:107
  176.3 1.2 fusion.120
  177.7 1.3 fusion.10
  190.2 4.7 %conditional.3 = ((f32[1,128,2,128]{1,3,2,0:T(8,128)S(1)}, f32[1,128,2]{1,2,0:T(2,128)S(1)}, f32[1,128,2]{1,2,0:T(2,128)S(1)})) conditional(s32[]{:T(128)} %bitcast.111, (f32[1,128,2,128]{1,3,2,0:T(8,128)S(1)}, f32[1,128,2]{1,2,0:T(2,128)S(1)}, f32[1,128,2]{1,2,0:T(2,128)S(1)}) %tuple.96, (pred[1]{0:T(512)(128)(4,1)}, s32[]{:T(128)}, ...), branch_computations={%region_3.3_spmd, %region_4.6_spmd.clone} | conditional | flops 68782224 | bytes 2977504 | solution.py:107
  192.3 1.2 fusion.120
  193.6 1.3 fusion.10
  217.5 4.7 %conditional.3 = ((f32[1,128,2,128]{1,3,2,0:T(8,128)S(1)}, f32[1,128,2]{1,2,0:T(2,128)S(1)}, f32[1,128,2]{1,2,0:T(2,128)S(1)})) conditional(s32[]{:T(128)} %bitcast.111, (f32[1,128,2,128]{1,3,2,0:T(8,128)S(1)}, f32[1,128,2]{1,2,0:T(2,128)S(1)}, f32[1,128,2]{1,2,0:T(2,128)S(1)}) %tuple.96, (pred[1]{0:T(512)(128)(4,1)}, s32[]{:T(128)}, ...), branch_computations={%region_3.3_spmd, %region_4.6_spmd.clone} | conditional | flops 68782224 | bytes 2977504 | solution.py:107
  219.5 1.2 fusion.120
  220.9 1.3 fusion.10
  223.1 1.2 convert_element_type.80
  224.3 132.2 %all-reduce.2.cloned.1.call-done = bf16[128,4096]{1,0:T(8,128)(2,1)} async-done(((bf16[128,4096]{1,0:T(8,128)(2,1)}), bf16[128,4096]{1,0:T(8,128)(2,1)}) %all-reduce.2.cloned.1.call-update) | async-done | bytes 1048592 | tf_op jit(solution)/shard_map/psum | solution.py:122
  356.5 1.5 convert_reduce_fusion
  358.1 1.7 multiply_reduce_fusion
  359.8 6.4 %convolution_convert_fusion = bf16[128,4096]{1,0:T(8,128)(2,1)} fusion(bf16[512,4096]{1,0:T(8,128)(2,1)} %param.22, bf16[4096,512]{1,0:T(8,128)(2,1)} %param.21, bf16[128,4096]{1,0:T(8,128)(2,1)S(1)} %copy-done.1, f32[4096]{0:T(1024)S(1)} %copy-done.3, f32[128]{0:T(128)S(1)} %add_rsqrt_fusion, f32[128]{0:T(128)S(1)} %broadcast_multiply_fusion), kind=kOutput, calls=%fused_computation.40 | convolution fusion | flops 1081147392 | bytes 10503168 | tf_op jit(solution)/shard_map/dot_general | solution.py:130
  366.2 0.7 copy.32
  367.0 1.6 convert_element_type.81
  368.5 63.9 %reduce-scatter.2.cloned.1.call-done = bf16[128,256]{1,0:T(8,128)(2,1)} async-done(((bf16[128,4096]{1,0:T(8,128)(2,1)}), bf16[128,256]{1,0:T(8,128)(2,1)}) %reduce-scatter.2.cloned.1.call-update) | async-done | bytes 65552 | tf_op jit(solution)/shard_map/reduce_scatter | solution.py:131
  432.5 1.7 select_convert_fusion
  (138 shorter events, 13.0 us)
Async XLA Ops:
  7.2 215.1 %copy-start = (bf16[256,4096]{1,0:T(8,128)(2,1)S(1)}, bf16[256,4096]{1,0:T(8,128)(2,1)}, u32[]{:S(2)}) copy-start(bf16[256,4096]{1,0:T(8,128)(2,1)} %param.20) | copy-start | bytes 6291460
  7.2 114.7 %all-gather.2.cloned.1.call-start = ((), (), s32[]{:S(2)}) async-start(), calls=%async_computation.1 | async-start | bytes 8912896 | tf_op jit(solution)/shard_map/all_gather | solution.py:85
  7.9 348.6 %all-reduce.2.cloned.1.call-start = ((), (), s32[]{:S(2)}) async-start(), calls=%async_computation.2 | async-start | bytes 2097152 | tf_op jit(solution)/shard_map/psum | solution.py:122
  134.4 8.8 %copy-start.4 = (s32[16]{0:T(128)S(1)}, s32[16]{0:T(128)}, u32[]{:S(2)}) copy-start(s32[16]{0:T(128)} %param.25) | copy-start | bytes 196
  222.2 0.8 copy-start.2
  224.3 135.5 %copy-start.3 = (f32[4096]{0:T(1024)S(1)}, f32[4096]{0:T(1024)}, u32[]{:S(2)}) copy-start(f32[4096]{0:T(1024)} %param.19) | copy-start | bytes 49156
  224.3 208.2 %reduce-scatter.2.cloned.1.call-start = ((), (), s32[]{:S(2)}) async-start(), calls=%async_computation.3 | async-start | bytes 1114112 | tf_op jit(solution)/shard_map/reduce_scatter | solution.py:131
  356.5 3.2 copy-start.1
Sparse Core Ops, SparseCore 0:
  10.4 111.4 all-gather.1
  224.4 132.0 all-reduce.1
  366.3 66.0 reduce-scatter.1
where the time goes:
time: 442 us; the launch traced here: 441 us
  waiting for transfers between devices  304 us (69%)
  loops' own time  58.2 us (13%)
  local copies, waits for them, and re-layouts  36.9 us (8%)
  matrix products  18.1 us (4%)
  between operations  13.9 us (3%)
  other arithmetic  9.68 us (2%)
    psum x1, waiting for transfers between devices, shards(): lax.psum(head_term.astype(jnp.bfloat16), 'mp').astype(jnp.float32)  132 us
    all_gather x1, waiting for transfers between devices, shards(): shard_piece = lax.all_gather(prefix_kv, 'req', axis=1, tiled=True)  107 us
    reduce_scatter x1, waiting for transfers between devices, shards(): lax.psum_scatter(projected.astype(jnp.bfloat16), 'mp', scatter_dimension=...  63.9 us
    another operation x1, loops' own time, shards(): result = lax.fori_loop(0, block_total, fold_step, own_part)  50.1 us
    reshape x1, local copies, waits for them, and re-layouts, shards(): blocks_here = shard_piece.reshape(2, block_total, KB, head_count, DH)  12.5 us
    unnamed x17, local copies, waits for them, and re-layouts  11.3 us
    dynamic_slice x16, local copies, waits for them, and re-layouts, fold_step(): logical = prefix_owner[block_index]  9.59 us
  transfers between devices with their start and end apart: 3, of which 3 were waited for; matrix products, arithmetic and copies ran while one was open for 2% of the time, Pallas kernels for 0%

commit v1 on v0

--- a/solution.py
+++ b/solution.py
@@ -2,6 +2,7 @@
 import jax.numpy as jnp
 from jax import lax
 from jax.sharding import PartitionSpec as P
+from jax.lax import all_to_all, axis_size
 
 H = 32
 DH = 128
@@ -82,7 +83,10 @@
         False,
     )
     key_offsets = jnp.arange(KB)
-    shard_piece = lax.all_gather(prefix_kv, "req", axis=1, tiled=True)
+    replace_values = lambda row_data, axis_key: jnp.concatenate(
+        all_to_all(jnp.stack([row_data] * axis_size(axis_key), axis=0), axis_key, 0, 0), 1
+    )
+    shard_piece = replace_values(prefix_kv, "req")
     block_total = shard_piece.shape[1] // KB
     blocks_here = shard_piece.reshape(2, block_total, KB, head_count, DH)
 

time: 442 us -> 516 us (1.17)
  waiting for transfers between devices: 304 us -> 373 us
  starting transfers between devices: 0.12 us -> 11.6 us
  local copies, waits for them, and re-layouts: 36.9 us -> 30.1 us
    all_to_all x0 -> x1, waiting for transfers between devices: none -> 179 us  [shards(): all_to_all(jnp.stack([row_data] * axis_size(axis_key), axis=0), axis_key,...]
    all_gather x1 -> x0, waiting for transfers between devices: 107 us -> none  [shards(): shard_piece = lax.all_gather(prefix_kv, 'req', axis=1, tiled=True)]
    reshape x1 -> x0, local copies, waits for them, and re-layouts: 12.5 us -> none  [shards(): blocks_here = shard_piece.reshape(2, block_total, KB, head_count, DH)]
    all_to_all x0 -> x1, starting transfers between devices: none -> 11.6 us  [shards(): all_to_all(jnp.stack([row_data] * axis_size(axis_key), axis=0), axis_key,...]
    unnamed x17 -> x26, local copies, waits for them, and re-layouts: 11.3 us -> 15 us
  transfers between devices with their start and end apart: 3 -> 3, of which waited for: 3 -> 3; matrix products, arithmetic and copies ran while one was open for 2% -> 1% of each run, Pallas kernels for 0% -> 0%
where the time goes in v1:
time: 516 us; the launch traced here: 515 us
  waiting for transfers between devices  373 us (72%)
  loops' own time  58.9 us (11%)
  local copies, waits for them, and re-layouts  30.1 us (6%)
  matrix products  17.3 us (3%)
  between operations  14.2 us (3%)
  starting transfers between devices  11.6 us (2%)
  other arithmetic  9.7 us (2%)
    all_to_all x1, waiting for transfers between devices, shards(): all_to_all(jnp.stack([row_data] * axis_size(axis_key), axis=0), axis_key,...  179 us
    psum x1, waiting for transfers between devices, shards(): lax.psum(head_term.astype(jnp.bfloat16), 'mp').astype(jnp.float32)  130 us
    reduce_scatter x1, waiting for transfers between devices, shards(): lax.psum_scatter(projected.astype(jnp.bfloat16), 'mp', scatter_dimension=...  63.8 us
    another operation x1, loops' own time, shards(): result = lax.fori_loop(0, block_total, fold_step, own_part)  51 us
    unnamed x26, local copies, waits for them, and re-layouts  15 us
    all_to_all x1, starting transfers between devices, shards(): all_to_all(jnp.stack([row_data] * axis_size(axis_key), axis=0), axis_key,...  11.6 us
  transfers between devices with their start and end apart: 3, of which 3 were waited for; matrix products, arithmetic and copies ran while one was open for 1% of the time, Pallas kernels for 0%

profile of v1, /device:TPU:6, one launch (start us, length us, event | category | flops | bytes accessed | tf_op | source)
XLA Modules:
  0.0 514.6 jit_solution(9502711887898466621)
XLA Ops:
  7.2 1.4 copy.41
  8.6 4.2 stack.2
  12.8 11.6 %all-to-all-start = ((bf16[16,2,512,256]{2,3,1,0:T(8,128)(2,1)}), bf16[16,2,512,256]{2,3,1,0:T(8,128)(2,1)}, u32[]{:S(2)}, u32[]{:S(2)}) async-start(bf16[16,2,512,256]{2,3,1,0:T(8,128)(2,1)} %stack.2), calls=%async_computation | async-start | bytes 16777216 | tf_op jit(solution)/shard_map/all_to_all | solution.py:87
  24.8 0.6 dynamic_slice.34
  25.4 0.6 iota_compare_fusion.1
  26.8 0.6 dynamic_slice.35
  27.6 179.4 %all-to-all-done = bf16[16,2,512,256]{2,3,1,0:T(8,128)(2,1)} async-done(((bf16[16,2,512,256]{2,3,1,0:T(8,128)(2,1)}), bf16[16,2,512,256]{2,3,1,0:T(8,128)(2,1)}, u32[]{:S(2)}, u32[]{:S(2)}) %all-to-all-start) | async-done | bytes 8388640 | tf_op jit(solution)/shard_map/all_to_all | solution.py:87
  207.0 11.9 %copy.45 = bf16[2,16,512,2,128]{4,2,3,1,0:T(8,128)(2,1)} copy(bf16[2,16,512,2,128]{2,4,3,0,1:T(8,128)(2,1)} %bitcast.26) | data formatting | bytes 16777216
  218.9 79.7 %while.20 = (s32[]{:T(128)}, f32[1,128,2,128]{1,3,2,0:T(8,128)S(1)}, f32[1,128,2]{1,2,0:T(2,128)S(1)}, f32[1,128,2]{1,2,0:T(2,128)S(1)}, s32[16]{0:T(128)S(1)}, ...) while((s32[]{:T(128)}, ...), condition=%wide.region_7.8_spmd.clone, body=%wide.region_2.7_spmd.clone.sunk | while | flops 68782248 | bytes 2980497 | solution.py:113
  226.5 4.7 conditional.3
  228.5 1.2 fusion.120
  229.9 1.3 fusion.10
  250.2 4.7 conditional.3
  252.3 1.2 fusion.120
  253.6 1.3 fusion.10
  254.9 0.6 dynamic_slice.54
  258.7 0.6 dynamic_slice.54
  266.3 4.7 conditional.3
  268.4 1.2 fusion.120
  269.7 1.3 fusion.10
  293.9 4.7 conditional.3
  295.9 1.2 fusion.120
  297.3 1.3 fusion.10
  299.5 1.2 convert_element_type.80
  300.7 129.6 %all-reduce.2.cloned.1.call-done = bf16[128,4096]{1,0:T(8,128)(2,1)} async-done(((bf16[128,4096]{1,0:T(8,128)(2,1)}), bf16[128,4096]{1,0:T(8,128)(2,1)}) %all-reduce.2.cloned.1.call-update) | async-done | bytes 1048592 | tf_op jit(solution)/shard_map/psum | solution.py:126
  430.3 1.5 convert_reduce_fusion
  431.9 1.7 multiply_reduce_fusion
  433.5 6.4 %convolution_convert_fusion = bf16[128,4096]{1,0:T(8,128)(2,1)} fusion(bf16[512,4096]{1,0:T(8,128)(2,1)} %param.22, bf16[4096,512]{1,0:T(8,128)(2,1)} %param.21, bf16[128,4096]{1,0:T(8,128)(2,1)S(1)} %copy-done.1, f32[4096]{0:T(1024)S(1)} %copy-done.5, f32[128]{0:T(128)S(1)} %add_rsqrt_fusion, f32[128]{0:T(128)S(1)} %broadcast_multiply_fusion), kind=kOutput, calls=%fused_computation.40 | convolution fusion | flops 1081147392 | bytes 10503168 | tf_op jit(solution)/shard_map/dot_general | solution.py:134
  440.0 0.7 copy.47
  440.8 1.5 convert_element_type.81
  442.3 63.8 %reduce-scatter.2.cloned.1.call-done = bf16[128,256]{1,0:T(8,128)(2,1)} async-done(((bf16[128,4096]{1,0:T(8,128)(2,1)}), bf16[128,256]{1,0:T(8,128)(2,1)}) %reduce-scatter.2.cloned.1.call-update) | async-done | bytes 65552 | tf_op jit(solution)/shard_map/reduce_scatter | solution.py:135
  506.1 1.7 select_convert_fusion
  (146 shorter events, 12.1 us)
Async XLA Ops:
  7.2 291.5 %copy-start = (bf16[256,4096]{1,0:T(8,128)(2,1)S(1)}, bf16[256,4096]{1,0:T(8,128)(2,1)}, u32[]{:S(2)}) copy-start(bf16[256,4096]{1,0:T(8,128)(2,1)} %param.20) | copy-start | bytes 6291460
  12.8 11.6 %copy-start.3 = (bf16[2,128,256]{2,1,0:T(8,128)(2,1)S(1)}, bf16[2,128,256]{2,1,0:T(8,128)(2,1)}, u32[]{:S(2)}) copy-start(bf16[2,128,256]{2,1,0:T(8,128)(2,1)} %param.16) | copy-start | bytes 393220
  12.8 11.9 %copy-start.2 = (bf16[128,256]{1,0:T(8,128)(2,1)S(1)}, bf16[128,256]{1,0:T(8,128)(2,1)}, u32[]{:S(2)}) copy-start(bf16[128,256]{1,0:T(8,128)(2,1)} %param.15) | copy-start | bytes 196612
  12.8 12.0 %copy-start.6 = (s32[16]{0:T(128)S(1)}, s32[16]{0:T(128)}, u32[]{:S(2)}) copy-start(s32[16]{0:T(128)} %param.23) | copy-start | bytes 196
  12.8 14.1 %copy-start.7 = (s32[16]{0:T(128)S(1)}, s32[16]{0:T(128)}, u32[]{:S(2)}) copy-start(s32[16]{0:T(128)} %param.24) | copy-start | bytes 196
  12.8 194.2 %all-to-all-start = ((bf16[16,2,512,256]{2,3,1,0:T(8,128)(2,1)}), bf16[16,2,512,256]{2,3,1,0:T(8,128)(2,1)}, u32[]{:S(2)}, u32[]{:S(2)}) async-start(bf16[16,2,512,256]{2,3,1,0:T(8,128)(2,1)} %stack.2), calls=%async_computation | async-start | bytes 16777216 | tf_op jit(solution)/shard_map/all_to_all | solution.py:87
  24.3 406.0 %all-reduce.2.cloned.1.call-start = ((), (), s32[]{:S(2)}) async-start(), calls=%async_computation.2 | async-start | bytes 2097152 | tf_op jit(solution)/shard_map/psum | solution.py:126
  207.0 11.9 %copy-start.8 = (s32[16]{0:T(128)S(1)}, s32[16]{0:T(128)}, u32[]{:S(2)}) copy-start(s32[16]{0:T(128)} %param.25) | copy-start | bytes 196
  298.6 0.8 copy-start.4
  300.7 132.9 %copy-start.5 = (f32[4096]{0:T(1024)S(1)}, f32[4096]{0:T(1024)}, u32[]{:S(2)}) copy-start(f32[4096]{0:T(1024)} %param.19) | copy-start | bytes 49156
  300.7 205.4 %reduce-scatter.2.cloned.1.call-start = ((), (), s32[]{:S(2)}) async-start(), calls=%async_computation.3 | async-start | bytes 1114112 | tf_op jit(solution)/shard_map/reduce_scatter | solution.py:135
  430.3 3.2 copy-start.1
Sparse Core Ops, SparseCore 0:
  300.8 129.4 all-reduce.1
  440.1 65.8 reduce-scatter.1
